TPU v7x, 512 devices: a whole 4x4x16 slice. The times are simulated.
512 devices in a mesh: blk: 64 (over x, z), head: 8 (over y, core).
Axes of the slice: x: 4, y: 4, z: 16, core: 2. Of those that a mesh axis runs over, the one named last changes fastest.
Arguments:
- acceptance_vector: bfloat16 [8192, 4096], P('blk', 'head'), may hold values from -6 to 6
- lookup_vector_array: bfloat16 [8192, 4096], P('blk', 'head'), may hold values from -2 to 2
- payload_vector_array: bfloat16 [8192, 4096], P('blk', 'head'), may hold values from -6 to 6
- raw_gating_signal: bfloat16 [8192, 4096], P('blk', 'head'), may hold values from -6 to 6
- raw_forgetting_rate: bfloat16 [8192, 4096], P('blk', 'head'), may hold values from -16 to 1
- current_reward_vector: float32 [4096], P('head'), may hold values from -1.5 to 1.5
- memory_following_query: bfloat16 [2, 4096, 64], P(None, 'head'), may hold values from -24 to 24
- group_layernorm_scaling: float32 [4096], P('head'), may hold values from 0.25 to 1.75
- closing_layernorm_scaling: float32 [4096], replicated, may hold values from 0.25 to 1.75
- skip_stream_input: bfloat16 [8192, 4096], P(('blk', 'head')), may hold values from -6 to 6
- closing_projection: bfloat16 [4096, 4096], P('head', 'blk'), may hold values from -0.09375 to 0.09375
- vocabulary_readout: bfloat16 [32768, 4096], P('blk'), may hold values from -15.625 to 15.625
- following_labels: int32 [8192], P(('blk', 'head')), may hold values from 0 to 32767
- response_indicator: int32 [8192], P(('blk', 'head')), may hold values 0 or 1
- baseline_logarithmic_likelihood: float32 [8192], P(('blk', 'head')), may hold values from -14 to -6
- rollout_for_segment: int32 [64], replicated, may hold values from 0 to 15, never falling along the last dimension, each value on 1 to 32 neighbouring positions
- query_text_for_rollout: int32 [16], replicated, may hold values from 0 to 1
Outputs:
- token_ratio: float32 [8192], P(('blk', 'head'))
- seq_ratio: float32 [16], replicated
Inputs may be any that keep to these rules, and one draw needn't show every extreme that they name: `rollout_for_segment`: sequences fill whole consecutive blocks, each 1 to 32 blocks, one exactly 32; ids start at 0 and rise by one at each new sequence.
All inputs are finite; a program needn't handle non-finite values. No bound on the sum of `response_indicator` on one device may be relied on, other than what follows from the above.
Results may differ from a plain program's by a relative error of at most 0.0017.
Values may be sent and summed in bfloat16 or wider, within the bound.
No kernel may reach another device: no remote copies, remote signals or barrier semaphores. Data moves between devices by JAX's collectives and lax.ppermute only.
A program may use at most 128 MiB of HBM per device.

v0:
```python
import jax
import jax.numpy as jnp
from jax import lax
from jax.sharding import PartitionSpec as P

GROUP_DIMENSION = 64
TOK_BLK = 128


def passed_along(value, axis, steps):
    count = lax.axis_size(axis)
    first, last = (max(0, -steps), min(count, count - steps))
    return lax.ppermute(value, axis, [(source, source + steps) for source in range(first, last)])


def joined(part, axis, combine):
    gathered = jax.tree.map(lambda a: lax.all_gather(a, axis), part)

    def take(source):
        return jax.tree.map(lambda a: lax.dynamic_index_in_dim(a, source, 0, False), gathered)

    return lax.fori_loop(
        1, lax.axis_size(axis), lambda source, state: combine(state, take(source)), take(0)
    )


def per_device(
    acceptance_vector,
    lookup_vector_array,
    payload_vector_array,
    raw_gating_signal,
    raw_forgetting_rate,
    current_reward_vector,
    memory_following_query,
    group_layernorm_scaling,
    closing_layernorm_scaling,
    skip_stream_input,
    closing_projection,
    vocabulary_readout,
    following_labels,
    response_indicator,
    baseline_logarithmic_likelihood,
    rollout_for_segment,
    query_text_for_rollout,
):
    n_blk = lax.axis_size("blk")
    blk_index = lax.axis_index("blk")
    rows, width = acceptance_vector.shape
    local_attention_groups = width // GROUP_DIMENSION
    sub = 16
    nsub = rows // sub
    highest = lax.Precision.HIGHEST

    def split(a):
        return (
            a.astype(jnp.float32)
            .reshape(nsub, sub, local_attention_groups, GROUP_DIMENSION)
            .transpose(0, 2, 1, 3)
        )

    inherited_memory = split(acceptance_vector)
    lookup_vectors = split(lookup_vector_array)
    vals = split(payload_vector_array)
    log_decay = -jnp.exp(split(raw_forgetting_rate))
    inclusive = jnp.cumsum(log_decay, axis=2)
    exclusive = inclusive - log_decay
    last = inclusive[:, :, -1, :]
    this_seq = rollout_for_segment[blk_index]
    prev_seq = rollout_for_segment[jnp.maximum(blk_index - 1, 0)]
    starts = jnp.logical_or(blk_index == 0, this_seq != prev_seq).astype(jnp.float32)
    prompt = (
        memory_following_query[query_text_for_rollout[this_seq]]
        .astype(jnp.float32)
        .reshape(local_attention_groups, GROUP_DIMENSION, GROUP_DIMENSION)
    )
    later = jnp.arange(sub)[:, None] > jnp.arange(sub)[None, :]
    spread = exclusive[:, :, :, None, :] - inclusive[:, :, None, :, :]
    weights = jnp.where(later[None, None, :, :, None], jnp.exp(jnp.minimum(spread, 0.0)), 0.0)
    scores = jnp.sum(
        inherited_memory[:, :, :, None, :] * lookup_vectors[:, :, None, :, :] * weights, axis=-1
    )
    group_current_reward = current_reward_vector.reshape(local_attention_groups, GROUP_DIMENSION)
    diagonal_term = jnp.sum(
        inherited_memory * lookup_vectors * group_current_reward[None, :, None, :], axis=-1
    )
    wkv = (
        jnp.einsum("nhts,nhsj->nhtj", scores, vals, precision=highest)
        + diagonal_term[..., None] * vals
    )
    keys_late = lookup_vectors * jnp.exp(last[:, :, None, :] - inclusive)
    delta = jnp.einsum("nhsi,nhsj->nhij", keys_late, vals, precision=highest)

    def advance(state, item):
        change, fall = item
        return (jnp.exp(fall)[:, :, None] * state + change, state)

    end_state, entering = lax.scan(advance, starts * prompt, (delta, last))
    wkv = wkv + jnp.einsum(
        "nhti,nhij->nhtj", inherited_memory * jnp.exp(exclusive), entering, precision=highest
    )
    block_fall = jnp.exp(jnp.sum(last, axis=0)) * (1.0 - starts)

    def relay_step(step, incoming):
        leaving = block_fall[:, :, None] * incoming + end_state
        return passed_along(leaving, "blk", 1)

    incoming = lax.fori_loop(0, n_blk // 2 - 1, relay_step, jnp.zeros_like(end_state))
    offsets = jnp.cumsum(last, axis=0) - last
    carried = inherited_memory * jnp.exp(exclusive + offsets[:, :, None, :])
    wkv = wkv + (1.0 - starts) * jnp.einsum("nhti,hij->nhtj", carried, incoming, precision=highest)
    mean = jnp.mean(wkv, axis=-1, keepdims=True)
    var = jnp.mean((wkv - mean) ** 2, axis=-1, keepdims=True)
    normal_h = (wkv - mean) / jnp.sqrt(var + 0.00064)
    normal_h = normal_h.transpose(0, 2, 1, 3).reshape(rows, width) * group_layernorm_scaling
    mixed = (normal_h * jax.nn.silu(raw_gating_signal.astype(jnp.float32))).astype(jnp.bfloat16)
    partial_out = jnp.dot(
        mixed,
        lax.all_gather(closing_projection, "blk", axis=1, tiled=True),
        preferred_element_type=jnp.float32,
    )
    own_rows = lax.psum_scatter(partial_out, "head", scatter_dimension=0, tiled=True)
    hidden = skip_stream_input.astype(jnp.float32) + own_rows
    hmean = jnp.mean(hidden, axis=-1, keepdims=True)
    hvar = jnp.mean((hidden - hmean) ** 2, axis=-1, keepdims=True)
    normed = ((hidden - hmean) / jnp.sqrt(hvar + 1e-05) * closing_layernorm_scaling).astype(
        jnp.bfloat16
    )
    local_rows = normed.shape[0]
    vocab_local = vocabulary_readout.shape[0]
    vocab_base = blk_index * vocab_local
    rows_n = lax.all_gather(normed, "blk", axis=0, tiled=True)
    rows_t = lax.all_gather(following_labels, "blk", axis=0, tiled=True)
    logits = lax.dot_general(
        rows_n, vocabulary_readout, (((1,), (1,)), ((), ())), preferred_element_type=jnp.float32
    )
    top = jnp.max(logits, axis=1)
    grand_sum = jnp.sum(jnp.exp(logits - top[:, None]), axis=1)
    entry = jnp.arange(vocab_local, dtype=jnp.int32)[None, :] + vocab_base
    picked = jnp.sum(jnp.where(entry == rows_t[:, None], logits, 0.0), axis=1)
    top, grand_sum, picked = tuple((new for new in (top, grand_sum, picked)))

    def join(first, second):
        peak = jnp.maximum(first[0], second[0])
        summed = first[1] * jnp.exp(first[0] - peak) + second[1] * jnp.exp(second[0] - peak)
        return (peak, summed, first[2] + second[2])

    top, grand_sum, picked = joined((top, grand_sum, picked), "blk", join)
    logp = picked - top - jnp.log(grand_sum)
    mine = lax.dynamic_slice_in_dim(logp, blk_index * local_rows, local_rows)
    token_ratio = response_indicator.astype(jnp.float32) * (mine - baseline_logarithmic_likelihood)
    seq_count = query_text_for_rollout.shape[0]
    marker = (jnp.arange(seq_count, dtype=jnp.int32) == this_seq).astype(jnp.float32)
    partial_seq = marker * (jnp.sum(token_ratio) / TOK_BLK)
    seq_ratio = lax.psum(partial_seq, ("blk", "head"))
    return (token_ratio, seq_ratio)


def solution(mesh):
    placed = (
        P("blk", "head"),
        P("blk", "head"),
        P("blk", "head"),
        P("blk", "head"),
        P("blk", "head"),
        P("head"),
        P(None, "head", None),
        P("head"),
        P(),
        P(("blk", "head"), None),
        P("head", "blk"),
        P("blk", None),
        P(("blk", "head")),
        P(("blk", "head")),
        P(("blk", "head")),
        P(),
        P(),
    )
    return jax.shard_map(
        per_device, mesh=mesh, in_specs=placed, out_specs=(P(("blk", "head")), P()), check_vma=False
    )
```

profile of v0, /device:TPU:1, one launch (start us, length us, event | category | flops | bytes accessed | tf_op | source)
XLA Modules:
  0.0 976.3 jit_solution(5648357997811550387)
XLA Ops:
  9.1 4.9 fusion.11
  25.3 7.4 while.41
  41.9 301.2 %while.42 = (s32[]{:T(128)}, f32[8,64,64]{2,1,0:T(8,128)S(1)}, f32[8,64]{1,0:T(8,128)S(1)}, f32[8,64,64]{2,1,0:T(8,128)S(1)}, s32[]{:T(128)}) while((s32[]{:T(128)}, f32[8,64,64]{2,1,0:T(8,128)S(1)}, f32[8,64]{1,0:T(8,128)S(1)}, f32[8,64,64]{2,1,0:T(8,128)S(1)}, s32[]{:T(128)}) %tuple.86), condition=%wide.region_7.8_spmd, body=%wide.region_6.7_spmd.sunk | while | flops 65538 | bytes 919653 | solution.py:107
  42.0 4.4 collective-permute-start
  46.4 3.6 collective-permute-done
  50.2 5.4 collective-permute-start
  55.6 3.6 collective-permute-done
  59.4 5.0 collective-permute-start
  64.4 3.6 collective-permute-done
  68.2 4.6 collective-permute-start
  72.8 3.7 collective-permute-done
  76.6 5.9 collective-permute-start
  86.2 5.3 collective-permute-start
  94.8 5.2 collective-permute-start
  100.1 4.4 collective-permute-done
  104.6 5.6 collective-permute-start
  110.2 4.0 collective-permute-done
  114.3 8.7 collective-permute-start
  123.0 8.9 collective-permute-done
  132.0 4.3 collective-permute-start
  136.3 7.5 collective-permute-done
  143.9 5.6 collective-permute-start
  149.6 7.7 collective-permute-done
  157.4 4.1 collective-permute-start
  161.5 4.4 collective-permute-done
  166.1 4.2 collective-permute-start
  173.7 4.6 collective-permute-start
  181.8 5.5 collective-permute-start
  190.7 5.3 collective-permute-start
  199.4 5.5 collective-permute-start
  208.4 5.0 collective-permute-start
  213.4 3.7 collective-permute-done
  217.2 5.3 collective-permute-start
  222.6 4.7 collective-permute-done
  227.5 5.5 collective-permute-start
  233.0 5.7 collective-permute-done
  238.9 6.0 collective-permute-start
  244.9 5.2 collective-permute-done
  250.2 4.8 collective-permute-start
  255.0 4.0 collective-permute-done
  259.2 4.1 collective-permute-start
  266.7 5.2 collective-permute-start
  275.3 5.3 collective-permute-start
  284.0 5.3 collective-permute-start
  292.8 5.0 collective-permute-start
  297.9 3.5 collective-permute-done
  301.5 5.3 collective-permute-start
  306.9 4.6 collective-permute-done
  311.6 5.6 collective-permute-start
  317.2 5.7 collective-permute-done
  323.1 6.0 collective-permute-start
  329.1 5.3 collective-permute-done
  334.6 4.6 collective-permute-start
  339.2 4.0 collective-permute-done
  345.3 5.0 fusion.26
  350.4 98.3 %reduce-scatter.2.cloned.1.call-done = f32[16,4096]{1,0:T(8,128)} async-done(((f32[128,4096]{1,0:T(8,128)}), f32[16,4096]{1,0:T(8,128)}) %reduce-scatter.2.cloned.1.call-update) | async-done | bytes 262160 | tf_op jit(solution)/shard_map/reduce_scatter | solution.py:121
  454.9 23.9 %all-reduce = s32[1024]{0:T(1024)S(1)} all-reduce(s32[1024]{0:T(1024)S(1)} %dynamic-update-slice), channel_id=1, replica_groups=mesh['blk'=64,'head'=8] {'blk'}, use_global_device_ids=true, to_apply=%add | all-reduce | flops 1024 | bytes 8192
  478.8 124.2 %all-gather.8.cloned.1.call-done = bf16[1024,4096]{1,0:T(8,128)(2,1)} async-done(((bf16[16,4096]{1,0:T(8,128)(2,1)}), bf16[1024,4096]{1,0:T(8,128)(2,1)}) %all-gather.8.cloned.1.call-update) | async-done | bytes 8388624 | tf_op jit(solution)/shard_map/all_gather | solution.py:131
  603.0 8.2 fusion.38
  611.8 61.3 %all-gather.1 = f32[65536]{0:T(1024)S(1)} all-gather(f32[1024]{0:T(1024)S(1)} %get-tuple-element.237), channel_id=3, replica_groups=mesh['blk'=64,'head'=8] {'blk'}, dimensions={0}, use_global_device_ids=true | all-gather | bytes 266240 | tf_op jit(solution)/shard_map/all_gather | solution.py:17
  673.2 63.6 %all-gather.2 = f32[65536]{0:T(1024)S(1)} all-gather(f32[1024]{0:T(1024)S(1)} %get-tuple-element.236), channel_id=4, replica_groups=mesh['blk'=64,'head'=8] {'blk'}, dimensions={0}, use_global_device_ids=true | all-gather | bytes 266240 | tf_op jit(solution)/shard_map/all_gather | solution.py:17
  736.8 63.0 %all-gather = f32[65536]{0:T(1024)S(1)} all-gather(f32[1024]{0:T(1024)S(1)} %get-tuple-element.289), channel_id=2, replica_groups=mesh['blk'=64,'head'=8] {'blk'}, dimensions={0}, use_global_device_ids=true | all-gather | bytes 266240 | tf_op jit(solution)/shard_map/all_gather | solution.py:17
  799.9 5.9 while.43
  808.4 161.3 %psum.7 = f32[16]{0:T(128)} all-reduce(f32[16]{0:T(128)S(1)} %compare_select_fusion), channel_id=1, replica_groups=mesh['blk'=64,'head'=8] {'blk','head'}, use_global_device_ids=true, to_apply=%region_20.21 | all-reduce | flops 16 | bytes 128 | tf_op jit(solution)/shard_map/psum | solution.py:154
  (417 shorter events, 77.4 us)
Async XLA Ops:
  7.2 7.9 copy-start.14
  7.2 10.5 %copy-start.17 = (s32[16]{0:T(128)S(1)}, s32[16]{0:T(128)}, u32[]{:S(2)}) copy-start(s32[16]{0:T(128)} %param.39) | copy-start | bytes 196
  7.2 14.3 %copy-start.10 = (bf16[2,512,64]{1,2,0:T(8,128)(2,1)S(1)}, bf16[2,512,64]{1,2,0:T(8,128)(2,1)}, u32[]{:S(2)}) copy-start(bf16[2,512,64]{1,2,0:T(8,128)(2,1)} %param.29) | copy-start | bytes 393220
  7.2 14.5 %copy-start.6 = (bf16[128,512]{1,0:T(8,128)(2,1)S(1)}, bf16[128,512]{1,0:T(8,128)(2,1)}, u32[]{:S(2)}) copy-start(bf16[128,512]{1,0:T(8,128)(2,1)} %param.23) | copy-start | bytes 393220
  7.2 338.0 %all-gather.6.cloned.1.call-start = ((), (), s32[]{:S(2)}) async-start(), calls=%async_computation.1 | async-start | bytes 4259840 | tf_op jit(solution)/shard_map/all_gather | solution.py:118
  7.9 440.7 %reduce-scatter.2.cloned.1.call-start = ((), (), s32[]{:S(2)}) async-start(), calls=%async_computation.2 | async-start | bytes 2359296 | tf_op jit(solution)/shard_map/reduce_scatter | solution.py:121
  9.0 12.9 %copy-start.7 = (bf16[128,512]{1,0:T(8,128)(2,1)S(1)}, bf16[128,512]{1,0:T(8,128)(2,1)}, u32[]{:S(2)}) copy-start(bf16[128,512]{1,0:T(8,128)(2,1)} %param.24) | copy-start | bytes 393220
  9.1 12.9 %copy-start.13 = (f32[512]{0:T(512)S(1)}, f32[512]{0:T(512)}, u32[]{:S(2)}) copy-start(f32[512]{0:T(512)} %param.28) | copy-start | bytes 6148
  9.1 13.0 %copy-start.8 = (bf16[128,512]{1,0:T(8,128)(2,1)S(1)}, bf16[128,512]{1,0:T(8,128)(2,1)}, u32[]{:S(2)}) copy-start(bf16[128,512]{1,0:T(8,128)(2,1)} %param.25) | copy-start | bytes 393220
  22.0 1.5 copy-start.1
  32.7 1.4 copy-start.2
  32.7 1.5 copy-start.3
  34.2 3.5 copy-start
  37.3 1.0 copy-start.4
  42.0 8.0 collective-permute-start
  50.2 9.0 collective-permute-start
  59.4 8.7 collective-permute-start
  68.2 8.3 collective-permute-start
  76.6 9.4 collective-permute-start
  86.2 8.5 collective-permute-start
  94.8 9.6 collective-permute-start
  104.6 9.6 collective-permute-start
  114.3 17.5 %collective-permute-start = (f32[8,64,64]{2,1,0:T(8,128)S(1)}, f32[8,64,64]{2,1,0:T(8,128)S(1)}, u32[]{:S(2)}, u32[]{:S(2)}) collective-permute-start(f32[8,64,64]{2,1,0:T(8,128)S(1)} %multiply_add_fusion.4), channel_id=1, source_target_pairs={{0,8},{8,16},{16,24},{24,32},{32,40},{40,48},{48,56},{56,64},{64,7... | collective-permute-start | bytes 393224 | tf_op jit(solution)/shard_map/while/body/eval_jaxpr/ppermute | solution.py:13
  132.0 11.8 %collective-permute-start = (f32[8,64,64]{2,1,0:T(8,128)S(1)}, f32[8,64,64]{2,1,0:T(8,128)S(1)}, u32[]{:S(2)}, u32[]{:S(2)}) collective-permute-start(f32[8,64,64]{2,1,0:T(8,128)S(1)} %multiply_add_fusion.4), channel_id=1, source_target_pairs={{0,8},{8,16},{16,24},{24,32},{32,40},{40,48},{48,56},{56,64},{64,7... | collective-permute-start | bytes 393224 | tf_op jit(solution)/shard_map/while/body/eval_jaxpr/ppermute | solution.py:13
  143.9 13.4 %collective-permute-start = (f32[8,64,64]{2,1,0:T(8,128)S(1)}, f32[8,64,64]{2,1,0:T(8,128)S(1)}, u32[]{:S(2)}, u32[]{:S(2)}) collective-permute-start(f32[8,64,64]{2,1,0:T(8,128)S(1)} %multiply_add_fusion.4), channel_id=1, source_target_pairs={{0,8},{8,16},{16,24},{24,32},{32,40},{40,48},{48,56},{56,64},{64,7... | collective-permute-start | bytes 393224 | tf_op jit(solution)/shard_map/while/body/eval_jaxpr/ppermute | solution.py:13
  157.4 8.5 collective-permute-start
  166.1 7.5 collective-permute-start
  173.7 7.9 collective-permute-start
  181.8 8.8 collective-permute-start
  190.7 8.6 collective-permute-start
  199.4 8.8 collective-permute-start
  208.4 8.7 collective-permute-start
  217.2 10.1 %collective-permute-start = (f32[8,64,64]{2,1,0:T(8,128)S(1)}, f32[8,64,64]{2,1,0:T(8,128)S(1)}, u32[]{:S(2)}, u32[]{:S(2)}) collective-permute-start(f32[8,64,64]{2,1,0:T(8,128)S(1)} %multiply_add_fusion.4), channel_id=1, source_target_pairs={{0,8},{8,16},{16,24},{24,32},{32,40},{40,48},{48,56},{56,64},{64,7... | collective-permute-start | bytes 393224 | tf_op jit(solution)/shard_map/while/body/eval_jaxpr/ppermute | solution.py:13
  227.5 11.3 %collective-permute-start = (f32[8,64,64]{2,1,0:T(8,128)S(1)}, f32[8,64,64]{2,1,0:T(8,128)S(1)}, u32[]{:S(2)}, u32[]{:S(2)}) collective-permute-start(f32[8,64,64]{2,1,0:T(8,128)S(1)} %multiply_add_fusion.4), channel_id=1, source_target_pairs={{0,8},{8,16},{16,24},{24,32},{32,40},{40,48},{48,56},{56,64},{64,7... | collective-permute-start | bytes 393224 | tf_op jit(solution)/shard_map/while/body/eval_jaxpr/ppermute | solution.py:13
  238.9 11.2 %collective-permute-start = (f32[8,64,64]{2,1,0:T(8,128)S(1)}, f32[8,64,64]{2,1,0:T(8,128)S(1)}, u32[]{:S(2)}, u32[]{:S(2)}) collective-permute-start(f32[8,64,64]{2,1,0:T(8,128)S(1)} %multiply_add_fusion.4), channel_id=1, source_target_pairs={{0,8},{8,16},{16,24},{24,32},{32,40},{40,48},{48,56},{56,64},{64,7... | collective-permute-start | bytes 393224 | tf_op jit(solution)/shard_map/while/body/eval_jaxpr/ppermute | solution.py:13
  250.2 8.8 collective-permute-start
  259.2 7.4 collective-permute-start
  266.7 8.4 collective-permute-start
  275.3 8.6 collective-permute-start
  284.0 8.6 collective-permute-start
  292.8 8.6 collective-permute-start
  301.5 9.9 %collective-permute-start = (f32[8,64,64]{2,1,0:T(8,128)S(1)}, f32[8,64,64]{2,1,0:T(8,128)S(1)}, u32[]{:S(2)}, u32[]{:S(2)}) collective-permute-start(f32[8,64,64]{2,1,0:T(8,128)S(1)} %multiply_add_fusion.4), channel_id=1, source_target_pairs={{0,8},{8,16},{16,24},{24,32},{32,40},{40,48},{48,56},{56,64},{64,7... | collective-permute-start | bytes 393224 | tf_op jit(solution)/shard_map/while/body/eval_jaxpr/ppermute | solution.py:13
  311.6 11.4 %collective-permute-start = (f32[8,64,64]{2,1,0:T(8,128)S(1)}, f32[8,64,64]{2,1,0:T(8,128)S(1)}, u32[]{:S(2)}, u32[]{:S(2)}) collective-permute-start(f32[8,64,64]{2,1,0:T(8,128)S(1)} %multiply_add_fusion.4), channel_id=1, source_target_pairs={{0,8},{8,16},{16,24},{24,32},{32,40},{40,48},{48,56},{56,64},{64,7... | collective-permute-start | bytes 393224 | tf_op jit(solution)/shard_map/while/body/eval_jaxpr/ppermute | solution.py:13
  323.1 11.3 %collective-permute-start = (f32[8,64,64]{2,1,0:T(8,128)S(1)}, f32[8,64,64]{2,1,0:T(8,128)S(1)}, u32[]{:S(2)}, u32[]{:S(2)}) collective-permute-start(f32[8,64,64]{2,1,0:T(8,128)S(1)} %multiply_add_fusion.4), channel_id=1, source_target_pairs={{0,8},{8,16},{16,24},{24,32},{32,40},{40,48},{48,56},{56,64},{64,7... | collective-permute-start | bytes 393224 | tf_op jit(solution)/shard_map/while/body/eval_jaxpr/ppermute | solution.py:13
  334.6 8.6 collective-permute-start
  344.4 0.9 copy-start.9
  344.4 0.9 copy-start.12
  350.3 98.3 %copy-start.5 = (bf16[16,4096]{1,0:T(8,128)(2,1)S(1)}, bf16[16,4096]{1,0:T(8,128)(2,1)}, u32[]{:S(2)}) copy-start(bf16[16,4096]{1,0:T(8,128)(2,1)} %param.32) | copy-start | bytes 393220
  350.3 100.6 %copy-start.11 = (f32[4096]{0:T(1024)S(1)}, f32[4096]{0:T(1024)}, u32[]{:S(2)}) copy-start(f32[4096]{0:T(1024)} %param.31) | copy-start | bytes 49156
  350.3 104.3 %copy-start.18 = (s32[16]{0:T(128)S(1)}, s32[16]{0:T(128)}, u32[]{:S(2)}) copy-start(s32[16]{0:T(128)} %param.35) | copy-start | bytes 196
  350.3 252.6 %all-gather.8.cloned.1.call-start = ((), (), s32[]{:S(2)}) async-start(), calls=%async_computation.3 | async-start | bytes 8519680 | tf_op jit(solution)/shard_map/all_gather | solution.py:131
  611.2 194.6 %copy-start.15 = (f32[16]{0:T(128)S(1)}, f32[16]{0:T(128)}, u32[]{:S(2)}) copy-start(f32[16]{0:T(128)} %param.37) | copy-start | bytes 196
  611.3 194.6 %copy-start.16 = (s32[16]{0:T(128)S(1)}, s32[16]{0:T(128)}, u32[]{:S(2)}) copy-start(s32[16]{0:T(128)} %param.36) | copy-start | bytes 196
Sparse Core Ops, SparseCore 0:
  11.0 147.0 all-gather.5
  350.5 98.1 reduce-scatter.1
  452.8 150.1 all-gather.7
where the time goes:
time: 978 us; the launch traced here: 976 us
  blocking collectives  373 us (38%)
  waiting for transfers between devices  357 us (37%)
  starting transfers between devices  163 us (17%)
  other arithmetic  24 us (2%)
  between operations  20.8 us (2%)
  matrix products  19.8 us (2%)
  local copies, waits for them, and re-layouts  14.7 us (2%)
    all_gather x3, blocking collectives, joined(): gathered = jax.tree.map(lambda a: lax.all_gather(a, axis), part)  188 us
    ppermute x31, starting transfers between devices, passed_along(): lax.ppermute(value, axis, [(source, source + steps) for source in range(f...  163 us
    psum x1, blocking collectives, per_device(): seq_ratio = lax.psum(partial_seq, ('blk', 'head'))  161 us
    ppermute x31, waiting for transfers between devices, passed_along(): lax.ppermute(value, axis, [(source, source + steps) for source in range(f...  134 us
    all_gather x1, waiting for transfers between devices, per_device(): rows_n = lax.all_gather(normed, 'blk', axis=0, tiled=True)  124 us
    reduce_scatter x1, waiting for transfers between devices, per_device(): lax.psum_scatter(partial_out, 'head', scatter_dimension=0, tiled=True)  98.3 us
    unnamed x1, blocking collectives  23.9 us
  transfers between devices with their start and end apart: 34, of which 33 were waited for; matrix products, arithmetic and copies ran while one was open for 4% of the time, Pallas kernels for 0%

commit v1 on v0

--- a/solution.py
+++ b/solution.py
@@ -43,6 +43,12 @@
     rollout_for_segment,
     query_text_for_rollout,
 ):
+
+    def pass_seats_all_here(packet, axis_key, ax_name):
+        for j0 in (axis_key, ax_name):
+            packet = jax.lax.psum(packet, axis_name=j0)
+        return packet
+
     n_blk = lax.axis_size("blk")
     blk_index = lax.axis_index("blk")
     rows, width = acceptance_vector.shape
@@ -151,7 +157,7 @@
     seq_count = query_text_for_rollout.shape[0]
     marker = (jnp.arange(seq_count, dtype=jnp.int32) == this_seq).astype(jnp.float32)
     partial_seq = marker * (jnp.sum(token_ratio) / TOK_BLK)
-    seq_ratio = lax.psum(partial_seq, ("blk", "head"))
+    seq_ratio = pass_seats_all_here(partial_seq, "blk", "head")
     return (token_ratio, seq_ratio)
 
 

time: 978 us -> 1030 us (1.053)
  blocking collectives: 373 us -> 427 us
    psum x1 -> x2, blocking collectives: 161 us -> 215 us  [pass_seats_all_here(): packet = jax.lax.psum(packet, axis_name=j0)]
  transfers between devices with their start and end apart: 34 -> 34, of which waited for: 33 -> 33; matrix products, arithmetic and copies ran while one was open for 4% -> 3% of each run, Pallas kernels for 0% -> 0%
where the time goes in v1:
time: 1030 us
  blocking collectives  427 us (41%)
  waiting for transfers between devices  357 us (35%)
  starting transfers between devices  163 us (16%)
  other arithmetic  24 us (2%)
  between operations  20.8 us (2%)
  matrix products  19.8 us (2%)
  local copies, waits for them, and re-layouts  14.7 us (1%)
    psum x2, blocking collectives, pass_seats_all_here(): packet = jax.lax.psum(packet, axis_name=j0)  215 us
    all_gather x3, blocking collectives, joined(): gathered = jax.tree.map(lambda a: lax.all_gather(a, axis), part)  188 us
    ppermute x31, starting transfers between devices, passed_along(): lax.ppermute(value, axis, [(source, source + steps) for source in range(f...  163 us
    ppermute x31, waiting for transfers between devices, passed_along(): lax.ppermute(value, axis, [(source, source + steps) for source in range(f...  134 us
    all_gather x1, waiting for transfers between devices, per_device(): rows_n = lax.all_gather(normed, 'blk', axis=0, tiled=True)  124 us
    reduce_scatter x1, waiting for transfers between devices, per_device(): lax.psum_scatter(partial_out, 'head', scatter_dimension=0, tiled=True)  98.3 us
    unnamed x1, blocking collectives  23.9 us
  transfers between devices with their start and end apart: 34, of which 33 were waited for; matrix products, arithmetic and copies ran while one was open for 3% of the time, Pallas kernels for 0%

profile of v1, /device:TPU:1, one launch (start us, length us, event | category | flops | bytes accessed | tf_op | source)
XLA Modules:
  0.0 1030.0 jit_solution(1791483548409085827)
XLA Ops:
  9.1 4.9 fusion.11
  25.3 7.4 while.41
  41.9 301.2 %while.42 = (s32[]{:T(128)}, f32[8,64,64]{2,1,0:T(8,128)S(1)}, f32[8,64]{1,0:T(8,128)S(1)}, f32[8,64,64]{2,1,0:T(8,128)S(1)}, s32[]{:T(128)}) while((s32[]{:T(128)}, f32[8,64,64]{2,1,0:T(8,128)S(1)}, f32[8,64]{1,0:T(8,128)S(1)}, f32[8,64,64]{2,1,0:T(8,128)S(1)}, s32[]{:T(128)}) %tuple.86), condition=%wide.region_7.8_spmd, body=%wide.region_6.7_spmd.sunk | while | flops 65538 | bytes 919653 | solution.py:113
  42.0 4.4 collective-permute-start
  46.4 3.6 collective-permute-done
  50.2 5.4 collective-permute-start
  55.6 3.6 collective-permute-done
  59.4 5.0 collective-permute-start
  64.4 3.6 collective-permute-done
  68.2 4.6 collective-permute-start
  72.8 3.7 collective-permute-done
  76.6 5.9 collective-permute-start
  86.2 5.3 collective-permute-start
  94.8 5.2 collective-permute-start
  100.1 4.4 collective-permute-done
  104.6 5.6 collective-permute-start
  110.2 4.0 collective-permute-done
  114.3 8.7 collective-permute-start
  123.0 8.9 collective-permute-done
  132.0 4.3 collective-permute-start
  136.3 7.5 collective-permute-done
  143.9 5.6 collective-permute-start
  149.6 7.7 collective-permute-done
  157.4 4.1 collective-permute-start
  161.5 4.4 collective-permute-done
  166.1 4.2 collective-permute-start
  173.7 4.6 collective-permute-start
  181.8 5.5 collective-permute-start
  190.7 5.3 collective-permute-start
  199.4 5.5 collective-permute-start
  208.4 5.0 collective-permute-start
  213.4 3.7 collective-permute-done
  217.2 5.3 collective-permute-start
  222.6 4.7 collective-permute-done
  227.5 5.5 collective-permute-start
  233.0 5.7 collective-permute-done
  238.9 6.0 collective-permute-start
  244.9 5.2 collective-permute-done
  250.2 4.8 collective-permute-start
  255.0 4.0 collective-permute-done
  259.2 4.1 collective-permute-start
  266.7 5.2 collective-permute-start
  275.3 5.3 collective-permute-start
  284.0 5.3 collective-permute-start
  292.8 5.0 collective-permute-start
  301.5 5.3 collective-permute-start
  306.9 4.6 collective-permute-done
  311.6 5.6 collective-permute-start
  317.2 5.7 collective-permute-done
  323.1 6.0 collective-permute-start
  329.1 5.3 collective-permute-done
  334.6 4.6 collective-permute-start
  339.2 4.0 collective-permute-done
  345.3 5.0 fusion.26
  350.4 98.3 %reduce-scatter.2.cloned.1.call-done = f32[16,4096]{1,0:T(8,128)} async-done(((f32[128,4096]{1,0:T(8,128)}), f32[16,4096]{1,0:T(8,128)}) %reduce-scatter.2.cloned.1.call-update) | async-done | bytes 262160 | tf_op jit(solution)/shard_map/reduce_scatter | solution.py:127
  454.9 23.9 %all-reduce = s32[1024]{0:T(1024)S(1)} all-reduce(s32[1024]{0:T(1024)S(1)} %dynamic-update-slice), channel_id=1, replica_groups=mesh['blk'=64,'head'=8] {'blk'}, use_global_device_ids=true, to_apply=%add | all-reduce | flops 1024 | bytes 8192
  478.8 124.2 %all-gather.8.cloned.1.call-done = bf16[1024,4096]{1,0:T(8,128)(2,1)} async-done(((bf16[16,4096]{1,0:T(8,128)(2,1)}), bf16[1024,4096]{1,0:T(8,128)(2,1)}) %all-gather.8.cloned.1.call-update) | async-done | bytes 8388624 | tf_op jit(solution)/shard_map/all_gather | solution.py:137
  603.0 8.2 fusion.38
  611.8 61.3 %all-gather.1 = f32[65536]{0:T(1024)S(1)} all-gather(f32[1024]{0:T(1024)S(1)} %get-tuple-element.237), channel_id=3, replica_groups=mesh['blk'=64,'head'=8] {'blk'}, dimensions={0}, use_global_device_ids=true | all-gather | bytes 266240 | tf_op jit(solution)/shard_map/all_gather | solution.py:17
  673.2 63.6 %all-gather.2 = f32[65536]{0:T(1024)S(1)} all-gather(f32[1024]{0:T(1024)S(1)} %get-tuple-element.236), channel_id=4, replica_groups=mesh['blk'=64,'head'=8] {'blk'}, dimensions={0}, use_global_device_ids=true | all-gather | bytes 266240 | tf_op jit(solution)/shard_map/all_gather | solution.py:17
  736.8 63.0 %all-gather = f32[65536]{0:T(1024)S(1)} all-gather(f32[1024]{0:T(1024)S(1)} %get-tuple-element.289), channel_id=2, replica_groups=mesh['blk'=64,'head'=8] {'blk'}, dimensions={0}, use_global_device_ids=true | all-gather | bytes 266240 | tf_op jit(solution)/shard_map/all_gather | solution.py:17
  799.9 5.9 while.43
  808.4 112.5 %psum.14 = f32[16]{0:T(128)S(1)} all-reduce(f32[16]{0:T(128)S(1)} %compare_select_fusion), channel_id=1, replica_groups=mesh['blk'=64,'head'=8] {'blk'}, use_global_device_ids=true, to_apply=%region_20.21 | all-reduce | flops 16 | bytes 128 | tf_op jit(solution)/shard_map/psum | solution.py:49
  920.9 102.6 %psum.15 = f32[16]{0:T(128)} all-reduce(f32[16]{0:T(128)S(1)} %psum.14), channel_id=1, replica_groups=mesh['blk'=64,'head'=8] {'head'}, use_global_device_ids=true, to_apply=%region_21.22 | all-reduce | flops 16 | bytes 128 | tf_op jit(solution)/shard_map/psum | solution.py:49
  (418 shorter events, 80.9 us)
Async XLA Ops:
  7.2 7.9 copy-start.14
  7.2 10.5 %copy-start.17 = (s32[16]{0:T(128)S(1)}, s32[16]{0:T(128)}, u32[]{:S(2)}) copy-start(s32[16]{0:T(128)} %param.39) | copy-start | bytes 196
  7.2 14.3 %copy-start.10 = (bf16[2,512,64]{1,2,0:T(8,128)(2,1)S(1)}, bf16[2,512,64]{1,2,0:T(8,128)(2,1)}, u32[]{:S(2)}) copy-start(bf16[2,512,64]{1,2,0:T(8,128)(2,1)} %param.29) | copy-start | bytes 393220
  7.2 14.5 %copy-start.6 = (bf16[128,512]{1,0:T(8,128)(2,1)S(1)}, bf16[128,512]{1,0:T(8,128)(2,1)}, u32[]{:S(2)}) copy-start(bf16[128,512]{1,0:T(8,128)(2,1)} %param.23) | copy-start | bytes 393220
  7.2 338.0 %all-gather.6.cloned.1.call-start = ((), (), s32[]{:S(2)}) async-start(), calls=%async_computation.1 | async-start | bytes 4259840 | tf_op jit(solution)/shard_map/all_gather | solution.py:124
  7.9 440.7 %reduce-scatter.2.cloned.1.call-start = ((), (), s32[]{:S(2)}) async-start(), calls=%async_computation.2 | async-start | bytes 2359296 | tf_op jit(solution)/shard_map/reduce_scatter | solution.py:127
  9.0 12.9 %copy-start.7 = (bf16[128,512]{1,0:T(8,128)(2,1)S(1)}, bf16[128,512]{1,0:T(8,128)(2,1)}, u32[]{:S(2)}) copy-start(bf16[128,512]{1,0:T(8,128)(2,1)} %param.24) | copy-start | bytes 393220
  9.1 12.9 %copy-start.13 = (f32[512]{0:T(512)S(1)}, f32[512]{0:T(512)}, u32[]{:S(2)}) copy-start(f32[512]{0:T(512)} %param.28) | copy-start | bytes 6148
  9.1 13.0 %copy-start.8 = (bf16[128,512]{1,0:T(8,128)(2,1)S(1)}, bf16[128,512]{1,0:T(8,128)(2,1)}, u32[]{:S(2)}) copy-start(bf16[128,512]{1,0:T(8,128)(2,1)} %param.25) | copy-start | bytes 393220
  22.0 1.5 copy-start.1
  32.7 1.4 copy-start.2
  32.7 1.5 copy-start.3
  34.2 3.5 copy-start
  37.3 1.0 copy-start.4
  42.0 8.0 collective-permute-start
  50.2 9.0 collective-permute-start
  59.4 8.7 collective-permute-start
  68.2 8.3 collective-permute-start
  76.6 9.4 collective-permute-start
  86.2 8.5 collective-permute-start
  94.8 9.6 collective-permute-start
  104.6 9.6 collective-permute-start
  114.3 17.5 %collective-permute-start = (f32[8,64,64]{2,1,0:T(8,128)S(1)}, f32[8,64,64]{2,1,0:T(8,128)S(1)}, u32[]{:S(2)}, u32[]{:S(2)}) collective-permute-start(f32[8,64,64]{2,1,0:T(8,128)S(1)} %multiply_add_fusion.4), channel_id=1, source_target_pairs={{0,8},{8,16},{16,24},{24,32},{32,40},{40,48},{48,56},{56,64},{64,7... | collective-permute-start | bytes 393224 | tf_op jit(solution)/shard_map/while/body/eval_jaxpr/ppermute | solution.py:13
  132.0 11.8 %collective-permute-start = (f32[8,64,64]{2,1,0:T(8,128)S(1)}, f32[8,64,64]{2,1,0:T(8,128)S(1)}, u32[]{:S(2)}, u32[]{:S(2)}) collective-permute-start(f32[8,64,64]{2,1,0:T(8,128)S(1)} %multiply_add_fusion.4), channel_id=1, source_target_pairs={{0,8},{8,16},{16,24},{24,32},{32,40},{40,48},{48,56},{56,64},{64,7... | collective-permute-start | bytes 393224 | tf_op jit(solution)/shard_map/while/body/eval_jaxpr/ppermute | solution.py:13
  143.9 13.4 %collective-permute-start = (f32[8,64,64]{2,1,0:T(8,128)S(1)}, f32[8,64,64]{2,1,0:T(8,128)S(1)}, u32[]{:S(2)}, u32[]{:S(2)}) collective-permute-start(f32[8,64,64]{2,1,0:T(8,128)S(1)} %multiply_add_fusion.4), channel_id=1, source_target_pairs={{0,8},{8,16},{16,24},{24,32},{32,40},{40,48},{48,56},{56,64},{64,7... | collective-permute-start | bytes 393224 | tf_op jit(solution)/shard_map/while/body/eval_jaxpr/ppermute | solution.py:13
  157.4 8.5 collective-permute-start
  166.1 7.5 collective-permute-start
  173.7 7.9 collective-permute-start
  181.8 8.8 collective-permute-start
  190.7 8.6 collective-permute-start
  199.4 8.8 collective-permute-start
  208.4 8.7 collective-permute-start
  217.2 10.1 collective-permute-start
  227.5 11.3 %collective-permute-start = (f32[8,64,64]{2,1,0:T(8,128)S(1)}, f32[8,64,64]{2,1,0:T(8,128)S(1)}, u32[]{:S(2)}, u32[]{:S(2)}) collective-permute-start(f32[8,64,64]{2,1,0:T(8,128)S(1)} %multiply_add_fusion.4), channel_id=1, source_target_pairs={{0,8},{8,16},{16,24},{24,32},{32,40},{40,48},{48,56},{56,64},{64,7... | collective-permute-start | bytes 393224 | tf_op jit(solution)/shard_map/while/body/eval_jaxpr/ppermute | solution.py:13
  238.9 11.2 %collective-permute-start = (f32[8,64,64]{2,1,0:T(8,128)S(1)}, f32[8,64,64]{2,1,0:T(8,128)S(1)}, u32[]{:S(2)}, u32[]{:S(2)}) collective-permute-start(f32[8,64,64]{2,1,0:T(8,128)S(1)} %multiply_add_fusion.4), channel_id=1, source_target_pairs={{0,8},{8,16},{16,24},{24,32},{32,40},{40,48},{48,56},{56,64},{64,7... | collective-permute-start | bytes 393224 | tf_op jit(solution)/shard_map/while/body/eval_jaxpr/ppermute | solution.py:13
  250.2 8.8 collective-permute-start
  259.2 7.4 collective-permute-start
  266.7 8.4 collective-permute-start
  275.3 8.6 collective-permute-start
  284.0 8.6 collective-permute-start
  292.8 8.6 collective-permute-start
  301.5 9.9 collective-permute-start
  311.6 11.4 %collective-permute-start = (f32[8,64,64]{2,1,0:T(8,128)S(1)}, f32[8,64,64]{2,1,0:T(8,128)S(1)}, u32[]{:S(2)}, u32[]{:S(2)}) collective-permute-start(f32[8,64,64]{2,1,0:T(8,128)S(1)} %multiply_add_fusion.4), channel_id=1, source_target_pairs={{0,8},{8,16},{16,24},{24,32},{32,40},{40,48},{48,56},{56,64},{64,7... | collective-permute-start | bytes 393224 | tf_op jit(solution)/shard_map/while/body/eval_jaxpr/ppermute | solution.py:13
  323.1 11.3 %collective-permute-start = (f32[8,64,64]{2,1,0:T(8,128)S(1)}, f32[8,64,64]{2,1,0:T(8,128)S(1)}, u32[]{:S(2)}, u32[]{:S(2)}) collective-permute-start(f32[8,64,64]{2,1,0:T(8,128)S(1)} %multiply_add_fusion.4), channel_id=1, source_target_pairs={{0,8},{8,16},{16,24},{24,32},{32,40},{40,48},{48,56},{56,64},{64,7... | collective-permute-start | bytes 393224 | tf_op jit(solution)/shard_map/while/body/eval_jaxpr/ppermute | solution.py:13
  334.6 8.6 collective-permute-start
  344.4 0.9 copy-start.9
  344.4 0.9 copy-start.12
  350.3 98.3 %copy-start.5 = (bf16[16,4096]{1,0:T(8,128)(2,1)S(1)}, bf16[16,4096]{1,0:T(8,128)(2,1)}, u32[]{:S(2)}) copy-start(bf16[16,4096]{1,0:T(8,128)(2,1)} %param.32) | copy-start | bytes 393220
  350.3 100.6 %copy-start.11 = (f32[4096]{0:T(1024)S(1)}, f32[4096]{0:T(1024)}, u32[]{:S(2)}) copy-start(f32[4096]{0:T(1024)} %param.31) | copy-start | bytes 49156
  350.3 104.3 %copy-start.18 = (s32[16]{0:T(128)S(1)}, s32[16]{0:T(128)}, u32[]{:S(2)}) copy-start(s32[16]{0:T(128)} %param.35) | copy-start | bytes 196
  350.3 252.6 %all-gather.8.cloned.1.call-start = ((), (), s32[]{:S(2)}) async-start(), calls=%async_computation.3 | async-start | bytes 8519680 | tf_op jit(solution)/shard_map/all_gather | solution.py:137
  611.2 194.6 %copy-start.15 = (f32[16]{0:T(128)S(1)}, f32[16]{0:T(128)}, u32[]{:S(2)}) copy-start(f32[16]{0:T(128)} %param.37) | copy-start | bytes 196
  611.3 194.6 %copy-start.16 = (s32[16]{0:T(128)S(1)}, s32[16]{0:T(128)}, u32[]{:S(2)}) copy-start(s32[16]{0:T(128)} %param.36) | copy-start | bytes 196
Sparse Core Ops, SparseCore 0:
  11.0 147.0 all-gather.5
  350.5 98.1 reduce-scatter.1
  452.8 150.1 all-gather.7
